TPU v7x, 256 devices: a whole 4x4x8 slice. The times are simulated.
256 devices in a mesh: seq: 64 (over x, z, core), tp: 4 (over y).
Axes of the slice: x: 4, y: 4, z: 8, core: 2. Of those that a mesh axis runs over, the one named last changes fastest.
Arguments:
- hidden_in: bfloat16 [16384, 1536], P('seq', 'tp'), may hold values from -6 to 6
- w_in_gate: float32 [1536, 3072], P('seq', 'tp'), may hold values from -0.15625 to 0.15625
- w_in_value: float32 [1536, 3072], P('seq', 'tp'), may hold values from -0.15625 to 0.15625
- w_in_shared: float32 [1536, 256], P('seq'), may hold values from -0.15625 to 0.15625
- w_in_step: float32 [1536, 48], P('seq', 'tp'), may hold values from -0.15625 to 0.15625
- conv_value: float32 [4, 3072], P(None, 'tp'), may hold values from -3 to 3
- conv_shared: float32 [4, 256], replicated, may hold values from -3 to 3
- dt_bias: float32 [48], P('tp'), may hold values from -4 to -2
- a_log: float32 [48], P('tp'), may hold values from -8 to 0
- skip_gain: float32 [48], P('tp'), may hold values from 0.6 to 4.8
- norm_gain: float32 [3072], P('tp'), may hold values from 0.1 to 1.9
- w_out: float32 [3072, 1536], P('tp', 'seq'), may hold values from -0.109375 to 0.109375
- prompt_lengths: int32 [8], replicated, may hold values from 1 to 8192, 16384 in all
- row_blocks: int32 [64], replicated, may hold values from 0 to 63, each once
Outputs:
- mixed_out: bfloat16 [16384, 1536], P('seq', 'tp')
Inputs may be any that keep to these rules, and one draw needn't show every extreme that they name: `prompt_lengths`: 8 lengths that sum to 16384, the longest exactly 8192. `row_blocks`: a permutation of the row blocks.
All inputs are finite; a program needn't handle non-finite values.
Results may differ from a plain program's by a relative error of at most 0.02.
Values may be sent and summed in bfloat16 or wider, within the bound.
No kernel may reach another device: no remote copies, remote signals or barrier semaphores. Data moves between devices by JAX's collectives and lax.ppermute only.
A program may use at most 128 MiB of HBM per device.

v0:
```python
import jax
import jax.numpy as jnp
from jax import lax
from jax.sharding import PartitionSpec as P

EPSILON = 1e-05
HIGHEST_PREC = lax.Precision.HIGHEST


def passed_along(block, axis, distance):
    devices = range(lax.axis_size(axis))
    route = [(i - distance, i) for i in devices if i - distance in devices]
    return lax.ppermute(block, axis, route)


def prefix_2(x, axis, combine, identity):
    count, here = (lax.axis_size(axis), lax.axis_index(axis))
    everything = jax.tree.map(
        lambda part, kind: lax.all_gather(part.astype(kind), axis), x, (jnp.bfloat16, jnp.bfloat16)
    )
    start = jax.tree.map(
        lambda part, zero: jnp.broadcast_to(jnp.asarray(zero, part.dtype), part.shape), x, identity
    )

    def turn(k, before):
        reached = k < here
        new = combine(
            before, jax.tree.map(lambda part, own: part[k].astype(own.dtype), everything, x)
        )
        return jax.tree.map(lambda a, b: jnp.where(reached, a, b), new, before)

    return lax.fori_loop(0, count, turn, start)


def segment_of(positions, doc_ends):
    return jnp.sum((positions[:, None] >= doc_ends[None, :]).astype(jnp.int32), axis=1)


def span_parts(values, b_half, c_half, steps_dt, decay_rates, segments, prev_seg):
    length = values.shape[0]
    b_rows = b_half.astype(jnp.float32)
    cumulative = jnp.cumsum(-steps_dt * decay_rates[None, :], axis=0)
    places = jnp.arange(length)
    causal = (places[:, None] >= places[None, :]) & (segments[:, None] == segments[None, :])
    gaps_log = jnp.where(causal[:, :, None], cumulative[:, None, :] - cumulative[None, :, :], 0.0)
    decays_in = jnp.where(causal[:, :, None], jnp.exp(gaps_log), 0.0)
    scores = jnp.dot(c_half, b_half.T, preferred_element_type=jnp.float32)
    weights = scores[:, :, None] * decays_in * steps_dt[None, :, :]
    intra_part = jnp.einsum("ijh,jhp->ihp", weights, values, precision=HIGHEST_PREC)
    carry_in = jnp.where((segments == prev_seg)[:, None], jnp.exp(cumulative), 0.0)
    tail_weight = (
        jnp.where(
            (segments == segments[-1])[:, None], jnp.exp(cumulative[-1][None, :] - cumulative), 0.0
        )
        * steps_dt
    )
    fresh_state = jnp.einsum("jh,jhp,jn->hpn", tail_weight, values, b_rows, precision=HIGHEST_PREC)
    keep_factor = jnp.where(segments[-1] == prev_seg, jnp.exp(cumulative[-1]), 0.0)
    return (intra_part, carry_in, fresh_state, keep_factor)


def combine(earlier, later):
    return (earlier[0] * later[0], later[0][:, None, None] * earlier[1] + later[1])


def on_device(
    hidden_in,
    w_in_gate,
    w_in_value,
    w_in_shared,
    w_in_step,
    conv_value,
    conv_shared,
    dt_bias,
    a_log,
    skip_gain,
    norm_gain,
    w_out,
    prompt_lengths,
    row_blocks,
):
    seq_count = lax.axis_size("seq")
    tokens_here = hidden_in.shape[0]
    edge_count = conv_value.shape[0] - 1
    gathered = lax.all_gather(hidden_in, "tp", axis=1, tiled=True)
    row_count = gathered.shape[0]
    model_width = gathered.shape[1]
    permuted = jnp.take(
        gathered.reshape(row_count, seq_count, model_width // seq_count), row_blocks, axis=1
    ).reshape(row_count, model_width)
    stored = (
        w_in_gate.astype(jnp.bfloat16),
        w_in_value.astype(jnp.bfloat16),
        w_in_shared.astype(jnp.bfloat16),
        w_in_step.astype(jnp.bfloat16),
    )
    pieces = (
        lax.all_gather(stored[0], "seq", axis=0, tiled=True),
        lax.all_gather(stored[1], "seq", axis=0, tiled=True),
        lax.all_gather(stored[2], "seq", axis=0, tiled=True),
        lax.all_gather(stored[3], "seq", axis=0, tiled=True),
    )
    projected = tuple(
        (
            jnp.dot(permuted, weight_piece, preferred_element_type=jnp.float32)
            for weight_piece in pieces
        )
    )
    gate_all, value_all, shared_all, raw_all = [result.astype(jnp.bfloat16) for result in projected]
    mixed_in = jnp.concatenate([value_all, shared_all], axis=1)
    edge_mix = passed_along(mixed_in[tokens_here - edge_count :], "seq", 1)
    doc_ends = jnp.cumsum(prompt_lengths)
    first_pos = lax.axis_index("seq") * tokens_here
    positions = first_pos + jnp.arange(tokens_here, dtype=jnp.int32)
    edge_positions = first_pos - edge_count + jnp.arange(edge_count, dtype=jnp.int32)
    segments = segment_of(positions, doc_ends)
    ext_segments = jnp.concatenate([segment_of(edge_positions, doc_ends), segments])
    ext_rows = jnp.concatenate([edge_mix, mixed_in], axis=0)
    kernel = jnp.concatenate([conv_value, conv_shared], axis=1)
    conv_sum = jnp.zeros(mixed_in.shape, jnp.float32)
    for tap_index in range(edge_count + 1):
        same_doc = (ext_segments[tap_index : tap_index + tokens_here] == segments)[:, None]
        conv_sum = conv_sum + jnp.where(
            same_doc,
            kernel[tap_index][None, :]
            * ext_rows[tap_index : tap_index + tokens_here].astype(jnp.float32),
            0.0,
        )
    convolved = jax.nn.silu(conv_sum).astype(jnp.bfloat16)
    local_inner = conv_value.shape[1]
    local_heads = dt_bias.shape[0]
    head_dim = local_inner // local_heads
    state_size = conv_shared.shape[1] // 2
    values = (
        convolved[:, :local_inner].astype(jnp.float32).reshape(tokens_here, local_heads, head_dim)
    )
    b_half = convolved[:, local_inner : local_inner + state_size]
    c_half = convolved[:, local_inner + state_size :]
    c_rows = c_half.astype(jnp.float32)
    steps_dt = jax.nn.softplus(raw_all.astype(jnp.float32) + dt_bias[None, :])
    decay_rates = jnp.exp(a_log)
    prev_first = segment_of(jnp.reshape(first_pos - 1, (1,)), doc_ends)[0]
    device_keep = jnp.ones((local_heads,), jnp.float32)
    device_state = jnp.zeros((local_heads, head_dim, state_size), jnp.float32)
    parts = span_parts(values, b_half, c_half, steps_dt, decay_rates, segments, prev_first)
    device_keep = parts[3] * device_keep
    device_state = parts[3][:, None, None] * device_state + parts[2]
    identity = (jnp.ones_like(device_keep), jnp.zeros_like(device_state))
    prefix = prefix_2((device_keep, device_state), "seq", combine, identity)
    carried = prefix[1]
    intra_part, carry_in, fresh_state, keep_factor = parts
    inter_part = (
        jnp.einsum("in,hpn->ihp", c_rows, carried, precision=HIGHEST_PREC) * carry_in[:, :, None]
    )
    outputs = intra_part + inter_part
    mixed_heads = outputs + skip_gain[None, :, None] * values
    gated = mixed_heads.reshape(tokens_here, local_inner) * jax.nn.silu(
        gate_all.astype(jnp.float32)
    )
    squares = jnp.sum(gated * gated, axis=1)
    square_total = lax.psum(squares, "tp")
    mean_square = square_total / (local_inner * lax.axis_size("tp"))
    normed = (gated * lax.rsqrt(mean_square + EPSILON)[:, None] * norm_gain[None, :]).astype(
        jnp.bfloat16
    )
    out_weight = w_out.astype(jnp.bfloat16)
    partial_terms = jnp.dot(
        normed,
        lax.all_gather(out_weight, "seq", axis=1, tiled=True),
        preferred_element_type=jnp.float32,
    )
    return lax.psum_scatter(
        partial_terms.astype(jnp.bfloat16), "tp", scatter_dimension=1, tiled=True
    )


def solution(mesh):
    return jax.shard_map(
        on_device,
        mesh=mesh,
        in_specs=(
            P("seq", "tp"),
            P("seq", "tp"),
            P("seq", "tp"),
            P("seq", None),
            P("seq", "tp"),
            P(None, "tp"),
            P(),
            P("tp"),
            P("tp"),
            P("tp"),
            P("tp"),
            P("tp", "seq"),
            P(),
            P(),
        ),
        out_specs=P("seq", "tp"),
        check_vma=False,
    )
```

profile of v0, /device:TPU:2, one launch (start us, length us, event | category | flops | bytes accessed | tf_op | source)
XLA Modules:
  0.0 420.0 jit_solution(3729731392679539498)
XLA Ops:
  6.5 1.5 convert_element_type.112
  9.6 1.1 copy.39
  13.0 46.7 %all-gather.1 = bf16[64,24,12]{1,2,0:T(8,128)(2,1)S(1)} all-gather(bf16[1,24,12]{1,2,0:T(8,128)(2,1)S(1)} %convert_bitcast_fusion), channel_id=1, replica_groups=mesh['seq'=64,'tp'=4] {'seq'}, dimensions={0}, use_global_device_ids=true | all-gather | bytes 37440 | tf_op jit(solution)/shard_map/all_gather | solution.py:101
  61.4 14.2 %all_gather.28 = bf16[256,1536]{0,1:T(8,128)(2,1)S(1)} all-gather(bf16[256,384]{0,1:T(8,128)(2,1)S(1)} %copy.39), channel_id=1, replica_groups=mesh['seq'=64,'tp'=4] {'tp'}, dimensions={1}, use_global_device_ids=true | all-gather | bytes 983040 | tf_op jit(solution)/shard_map/all_gather | solution.py:85
  80.0 48.3 %all_gather.30 = bf16[1536,256]{1,0:T(8,128)(2,1)S(1)} all-gather(bf16[24,256]{1,0:T(8,128)(2,1)S(1)} %convert_element_type.114), channel_id=1, replica_groups=mesh['seq'=64,'tp'=4] {'seq'}, dimensions={0}, use_global_device_ids=true | all-gather | bytes 798720 | tf_op jit(solution)/shard_map/all_gather | solution.py:100
  128.3 1.3 broadcast_compare_fusion
  130.1 2.5 convolution_convert_fusion.2
  132.6 2.3 collective-permute-start
  134.9 4.8 %collective-permute-done = bf16[3,1024]{1,0:T(4,128)(2,1)S(1)} collective-permute-done((bf16[3,1024]{1,0:T(4,128)(2,1)S(1)}, bf16[3,1024]{1,0:T(4,128)(2,1)S(1)}, u32[]{:S(2)}, u32[]{:S(2)}) %collective-permute-start) | collective-permute-done | bytes 6176 | tf_op jit(solution)/shard_map/ppermute | solution.py:13
  140.9 1.2 fusion.20
  143.9 38.1 %all-gather.2 = bf16[64,1,12]{2,1,0:T(2,128)(2,1)S(1)} all-gather(bf16[1,1,12]{2,1,0:T(2,128)(2,1)S(1)} %bitcast.96), channel_id=1, replica_groups=mesh['seq'=64,'tp'=4] {'seq'}, dimensions={0}, use_global_device_ids=true | all-gather | bytes 1560 | tf_op jit(solution)/shard_map/all_gather | solution.py:19
  182.2 3.6 fusion.14
  185.8 43.4 %all-gather.14.cloned.1.call-done = bf16[768,64,128]{2,1,0:T(8,128)(2,1)} async-done(((bf16[12,64,128]{2,1,0:T(8,128)(2,1)}), bf16[768,64,128]{2,1,0:T(8,128)(2,1)}) %all-gather.14.cloned.1.call-update) | async-done | bytes 12582928 | tf_op jit(solution)/shard_map/all_gather | solution.py:19
  229.1 70.1 %while.14 = (s32[]{:T(128)}, f32[12,64,128]{2,1,0:T(8,128)S(1)}, s32[]{:T(128)}, bf16[64,12]{1,0:T(8,128)(2,1)S(1)}, bf16[64,12,64,128]{3,2,1,0:T(8,128)(2,1)}, /*index=5*/s32[]{:T(128)}, s32[]{:T(128)}) while((s32[]{:T(128)}, f32[12,64,128]{2,1,0:T(8,128)S(1)}, s32[]{:T(128)}, bf16[64,12]{1,0:T(8,128)(2,1)S(1)}, ...), condition=%wide.region_7.8_spmd.clone, body=%wide.region_6.7_spmd.clone.sunk | while | flops 491536 | bytes 983265 | solution.py:32
  229.2 1.1 fusion.58
  230.2 1.1 fusion.58
  231.3 1.1 fusion.58
  233.5 1.1 fusion.58
  234.6 1.1 fusion.58
  235.7 1.1 fusion.58
  236.8 1.1 fusion.58
  237.9 1.1 fusion.58
  239.0 1.1 fusion.58
  240.1 1.1 fusion.58
  241.2 1.1 fusion.58
  242.3 1.1 fusion.58
  244.5 1.1 fusion.58
  245.6 1.1 fusion.58
  246.7 1.1 fusion.58
  247.7 1.1 fusion.58
  248.8 1.1 fusion.58
  251.0 1.1 fusion.58
  265.3 1.1 fusion.58
  278.4 1.1 fusion.58
  283.9 1.1 fusion.58
  287.2 1.1 fusion.58
  294.9 1.1 fusion.58
  296.0 1.1 fusion.58
  298.2 1.1 fusion.58
  299.3 1.6 fusion.18
  301.2 5.5 %all-gather.10.cloned.1.call-done = bf16[1536,768]{1,0:T(8,128)(2,1)} async-done(((bf16[24,768]{1,0:T(8,128)(2,1)}), bf16[1536,768]{1,0:T(8,128)(2,1)}) %all-gather.10.cloned.1.call-update) | async-done | bytes 2359312 | tf_op jit(solution)/shard_map/all_gather | solution.py:98
  306.7 2.7 multiply_reduce_fusion
  309.4 10.5 %psum.7 = f32[256]{0:T(256)S(1)} all-reduce(f32[256]{0:T(256)S(1)} %get-tuple-element.160), channel_id=1, replica_groups=mesh['seq'=64,'tp'=4] {'tp'}, use_global_device_ids=true, to_apply=%region_9.10 | all-reduce | flops 256 | bytes 2048 | tf_op jit(solution)/shard_map/psum | solution.py:161
  319.8 64.6 %all-gather.12.cloned.1.call-done = bf16[768,1536]{0,1:T(8,128)(2,1)} async-done(((bf16[768,24]{0,1:T(8,128)(2,1)}), bf16[768,1536]{0,1:T(8,128)(2,1)}) %all-gather.12.cloned.1.call-update) | async-done | bytes 2359312 | tf_op jit(solution)/shard_map/all_gather | solution.py:169
  384.4 2.5 convolution_convert_fusion
  386.9 1.2 copy.50
  388.1 23.7 %reduce-scatter.4.cloned.1.call-done = bf16[384,256]{1,0:T(8,128)(2,1)} async-done(((bf16[1536,256]{1,0:T(8,128)(2,1)}), bf16[384,256]{1,0:T(8,128)(2,1)}) %reduce-scatter.4.cloned.1.call-update) | async-done | bytes 196624
  411.8 1.7 copy.51
  (180 shorter events, 54.2 us)
Async XLA Ops:
  6.5 123.6 %all-gather.8.cloned.1.call-start = ((), (), s32[]{:S(2)}) async-start(), calls=%async_computation.1 | async-start | bytes 2396160 | tf_op jit(solution)/shard_map/all_gather | solution.py:99
  8.1 221.1 %all-gather.14.cloned.1.call-start = ((), (), s32[]{:S(2)}) async-start(), calls=%async_computation.4 | async-start | bytes 12779520 | tf_op jit(solution)/shard_map/all_gather | solution.py:19
  75.6 0.9 copy-start.5
  76.2 3.6 copy-start.2
  76.2 3.6 copy-start.4
  132.6 7.1 %collective-permute-start = (bf16[3,1024]{1,0:T(4,128)(2,1)S(1)}, bf16[3,1024]{1,0:T(4,128)(2,1)S(1)}, u32[]{:S(2)}, u32[]{:S(2)}) collective-permute-start(bf16[3,1024]{1,0:T(4,128)(2,1)S(1)} %fusion.40), channel_id=1, source_target_pairs={{0,4},{4,8},{8,12},{12,16},{16,20},{20,24},{24,28},{28,32},{32,36}... | collective-permute-start | bytes 18440 | tf_op jit(solution)/shard_map/ppermute | solution.py:13
  139.9 2.3 copy-start
  139.9 3.1 copy-start.1
  142.2 164.5 %all-gather.10.cloned.1.call-start = ((), (), s32[]{:S(2)}) async-start(), calls=%async_computation.2 | async-start | bytes 2396160 | tf_op jit(solution)/shard_map/all_gather | solution.py:98
  142.9 241.5 %all-gather.12.cloned.1.call-start = ((), (), s32[]{:S(2)}) async-start(), calls=%async_computation.3 | async-start | bytes 2396160 | tf_op jit(solution)/shard_map/all_gather | solution.py:169
  143.6 268.2 %reduce-scatter.4.cloned.1.call-start = ((), (), s32[]{:S(2)}) async-start(), calls=%async_computation.5 | async-start | bytes 983040
  229.1 70.1 %copy-start.6 = (f32[12]{0:T(128)S(1)}, f32[12]{0:T(128)}, u32[]{:S(2)}) copy-start(f32[12]{0:T(128)} %param.25) | copy-start | bytes 148
  301.2 83.2 %copy-start.3 = (f32[768]{0:T(1024)S(1)}, f32[768]{0:T(1024)}, u32[]{:S(2)}) copy-start(f32[768]{0:T(1024)} %param.26) | copy-start | bytes 9220
Sparse Core Ops, SparseCore 0:
  10.1 79.4 all-gather.7
  142.3 86.8 all-gather.13
  231.8 74.7 all-gather.9
  309.2 75.1 all-gather.11
  388.2 23.5 reduce-scatter.3
where the time goes:
time: 422 us; the launch traced here: 420 us
  blocking collectives  158 us (37%)
  waiting for transfers between devices  142 us (34%)
  other arithmetic  79 us (19%)
  matrix products  14.9 us (4%)
  between operations  14.6 us (3%)
  local copies, waits for them, and re-layouts  7.21 us (2%)
    select_n x64, other arithmetic, turn(): return jax.tree.map(lambda a, b: jnp.where(reached, a, b), new, before)  67.4 us
    all_gather x1, waiting for transfers between devices, on_device(): lax.all_gather(out_weight, 'seq', axis=1, tiled=True)  64.6 us
    all_gather x1, blocking collectives, on_device(): lax.all_gather(stored[2], 'seq', axis=0, tiled=True)  48.3 us
    all_gather x1, blocking collectives, on_device(): lax.all_gather(stored[3], 'seq', axis=0, tiled=True)  46.7 us
    all_gather x1, waiting for transfers between devices, prefix_2(): lax.all_gather(part.astype(kind), axis)  43.4 us
    all_gather x1, blocking collectives, prefix_2(): lax.all_gather(part.astype(kind), axis)  38.1 us
    unnamed x6, waiting for transfers between devices  23.8 us
    all_gather x1, blocking collectives, on_device(): gathered = lax.all_gather(hidden_in, 'tp', axis=1, tiled=True)  14.2 us
  transfers between devices with their start and end apart: 6, of which 5 were waited for; matrix products, arithmetic and copies ran while one was open for 21% of the time, Pallas kernels for 0%

commit v1 on v0

--- a/solution.py
+++ b/solution.py
@@ -2,6 +2,7 @@
 import jax.numpy as jnp
 from jax import lax
 from jax.sharding import PartitionSpec as P
+from jax.lax import axis_index, axis_size, ppermute
 
 EPSILON = 1e-05
 HIGHEST_PREC = lax.Precision.HIGHEST
@@ -82,7 +83,28 @@
     seq_count = lax.axis_size("seq")
     tokens_here = hidden_in.shape[0]
     edge_count = conv_value.shape[0] - 1
-    gathered = lax.all_gather(hidden_in, "tp", axis=1, tiled=True)
+    vec_out, out_arr, state_now = (axis_size("tp"), axis_index("tp"), hidden_in.shape[1])
+    row_list = tuple(
+        (i0 * vec_out if hop_no == 1 else i0 for hop_no, i0 in enumerate(hidden_in.shape))
+    )
+    piece_next = passed = hidden_in
+    gathered = lax.dynamic_update_slice_in_dim(
+        jnp.zeros(row_list, hidden_in.dtype), hidden_in, out_arr * state_now, axis=1
+    )
+    for it in [*range(1, vec_out // 2 + 1)]:
+        piece_next = ppermute(
+            piece_next, "tp", tuple(((hop_no, (hop_no + 1) % vec_out) for hop_no in range(vec_out)))
+        )
+        gathered = lax.dynamic_update_slice_in_dim(
+            gathered, piece_next, (out_arr - it) % vec_out * state_now, axis=1
+        )
+        if 2 * it < vec_out:
+            passed = ppermute(
+                passed, "tp", tuple(((hop_no, (hop_no - 1) % vec_out) for hop_no in range(vec_out)))
+            )
+            gathered = lax.dynamic_update_slice_in_dim(
+                gathered, passed, (out_arr + it) % vec_out * state_now, axis=1
+            )
     row_count = gathered.shape[0]
     model_width = gathered.shape[1]
     permuted = jnp.take(

time: 422 us -> 418 us (level)
  blocking collectives: 158 us -> 143 us
  waiting for transfers between devices: 142 us -> 148 us
    all_gather x1 -> x0, blocking collectives: 14.2 us -> none  [on_device(): gathered = lax.all_gather(hidden_in, 'tp', axis=1, tiled=True)]
    ppermute x0 -> x3, waiting for transfers between devices: none -> 7.96 us  [the longest x2 7.95 us: on_device(): ppermute(piece_next, 'tp', tuple(((hop_no, (hop_no + 1) % vec_out) for ho...]
  transfers between devices with their start and end apart: 6 -> 9, of which waited for: 5 -> 6; matrix products, arithmetic and copies ran while one was open for 21% -> 22% of each run, Pallas kernels for 0% -> 0%
where the time goes in v1:
time: 418 us; the launch traced here: 416 us
  waiting for transfers between devices  148 us (35%)
  blocking collectives  143 us (34%)
  other arithmetic  78.4 us (19%)
  matrix products  14.9 us (4%)
  between operations  14.7 us (4%)
  local copies, waits for them, and re-layouts  8.74 us (2%)
  starting transfers between devices  5.84 us (1%)
    select_n x64, other arithmetic, turn(): return jax.tree.map(lambda a, b: jnp.where(reached, a, b), new, before)  67.5 us
    all_gather x1, waiting for transfers between devices, on_device(): lax.all_gather(out_weight, 'seq', axis=1, tiled=True)  64.6 us
    all_gather x1, blocking collectives, on_device(): lax.all_gather(stored[2], 'seq', axis=0, tiled=True)  48.3 us
    all_gather x1, blocking collectives, on_device(): lax.all_gather(stored[3], 'seq', axis=0, tiled=True)  46.8 us
    all_gather x1, waiting for transfers between devices, prefix_2(): lax.all_gather(part.astype(kind), axis)  40.9 us
    all_gather x1, blocking collectives, prefix_2(): lax.all_gather(part.astype(kind), axis)  37.9 us
    unnamed x6, waiting for transfers between devices  23.9 us
    psum x1, blocking collectives, on_device(): square_total = lax.psum(squares, 'tp')  10.5 us
  transfers between devices with their start and end apart: 9, of which 6 were waited for; matrix products, arithmetic and copies ran while one was open for 22% of the time, Pallas kernels for 0%

profile of v1, /device:TPU:2, one launch (start us, length us, event | category | flops | bytes accessed | tf_op | source)
XLA Modules:
  0.0 415.8 jit_solution(4783606770137094219)
XLA Ops:
  6.5 1.5 convert_element_type.112
  8.1 1.1 copy.43
  9.2 1.7 collective-permute-start
  10.8 1.7 collective-permute-start.1
  14.1 46.8 %all-gather.1 = bf16[64,24,12]{1,2,0:T(8,128)(2,1)S(1)} all-gather(bf16[1,24,12]{1,2,0:T(8,128)(2,1)S(1)} %convert_bitcast_fusion), channel_id=1, replica_groups=mesh['seq'=64,'tp'=4] {'seq'}, dimensions={0}, use_global_device_ids=true | all-gather | bytes 37440 | tf_op jit(solution)/shard_map/all_gather | solution.py:123
  67.5 48.3 %all_gather.26 = bf16[1536,256]{1,0:T(8,128)(2,1)S(1)} all-gather(bf16[24,256]{1,0:T(8,128)(2,1)S(1)} %convert_element_type.114), channel_id=1, replica_groups=mesh['seq'=64,'tp'=4] {'seq'}, dimensions={0}, use_global_device_ids=true | all-gather | bytes 798720 | tf_op jit(solution)/shard_map/all_gather | solution.py:122
  115.8 1.3 broadcast_compare_fusion
  117.7 8.0 %collective-permute-done.2 = bf16[256,384]{0,1:T(8,128)(2,1)S(1)} collective-permute-done((bf16[256,384]{0,1:T(8,128)(2,1)S(1)}, bf16[256,384]{0,1:T(8,128)(2,1)S(1)}, u32[]{:S(2)}, u32[]{:S(2)}) %collective-permute-start.2) | collective-permute-done | bytes 196640 | tf_op jit(solution)/shard_map/ppermute | solution.py:95
  128.5 2.5 convolution_convert_fusion.2
  131.0 1.9 collective-permute-start.3
  132.9 5.1 %collective-permute-done.3 = bf16[3,1024]{1,0:T(4,128)(2,1)S(1)} collective-permute-done((bf16[3,1024]{1,0:T(4,128)(2,1)S(1)}, bf16[3,1024]{1,0:T(4,128)(2,1)S(1)}, u32[]{:S(2)}, u32[]{:S(2)}) %collective-permute-start.3) | collective-permute-done | bytes 6176 | tf_op jit(solution)/shard_map/ppermute | solution.py:14
  139.3 1.2 fusion.20
  142.3 37.9 %all-gather.2 = bf16[64,1,12]{2,1,0:T(2,128)(2,1)S(1)} all-gather(bf16[1,1,12]{2,1,0:T(2,128)(2,1)S(1)} %bitcast.96), channel_id=1, replica_groups=mesh['seq'=64,'tp'=4] {'seq'}, dimensions={0}, use_global_device_ids=true | all-gather | bytes 1560 | tf_op jit(solution)/shard_map/all_gather | solution.py:20
  180.4 3.6 fusion.14
  184.0 40.9 %all-gather.14.cloned.1.call-done = bf16[768,64,128]{2,1,0:T(8,128)(2,1)} async-done(((bf16[12,64,128]{2,1,0:T(8,128)(2,1)}), bf16[768,64,128]{2,1,0:T(8,128)(2,1)}) %all-gather.14.cloned.1.call-update) | async-done | bytes 12582928 | tf_op jit(solution)/shard_map/all_gather | solution.py:20
  224.8 70.1 %while.14 = (s32[]{:T(128)}, f32[12,64,128]{2,1,0:T(8,128)S(1)}, s32[]{:T(128)}, bf16[64,12]{1,0:T(8,128)(2,1)S(1)}, bf16[64,12,64,128]{3,2,1,0:T(8,128)(2,1)}, /*index=5*/s32[]{:T(128)}, s32[]{:T(128)}) while((s32[]{:T(128)}, f32[12,64,128]{2,1,0:T(8,128)S(1)}, s32[]{:T(128)}, bf16[64,12]{1,0:T(8,128)(2,1)S(1)}, ...), condition=%wide.region_7.8_spmd.clone, body=%wide.region_6.7_spmd.clone.sunk | while | flops 491536 | bytes 983265 | solution.py:33
  224.9 1.1 fusion.58
  225.9 1.1 fusion.58
  227.0 1.1 fusion.58
  228.1 1.1 fusion.58
  229.2 1.1 fusion.58
  230.3 1.1 fusion.58
  231.4 1.1 fusion.58
  232.5 1.1 fusion.58
  233.6 1.1 fusion.58
  234.7 1.1 fusion.58
  235.8 1.1 fusion.58
  236.9 1.1 fusion.58
  238.0 1.1 fusion.58
  243.4 1.1 fusion.58
  246.7 1.1 fusion.58
  250.0 1.1 fusion.58
  260.9 1.1 fusion.58
  274.1 1.1 fusion.58
  279.6 1.1 fusion.58
  282.9 1.1 fusion.58
  290.6 1.1 fusion.58
  291.7 1.1 fusion.58
  293.9 1.1 fusion.58
  294.9 1.6 fusion.18
  296.9 5.5 %all-gather.10.cloned.1.call-done = bf16[1536,768]{1,0:T(8,128)(2,1)} async-done(((bf16[24,768]{1,0:T(8,128)(2,1)}), bf16[1536,768]{1,0:T(8,128)(2,1)}) %all-gather.10.cloned.1.call-update) | async-done | bytes 2359312 | tf_op jit(solution)/shard_map/all_gather | solution.py:120
  302.4 2.7 multiply_reduce_fusion
  305.0 10.5 %psum.7 = f32[256]{0:T(256)S(1)} all-reduce(f32[256]{0:T(256)S(1)} %get-tuple-element.160), channel_id=1, replica_groups=mesh['seq'=64,'tp'=4] {'tp'}, use_global_device_ids=true, to_apply=%region_9.10 | all-reduce | flops 256 | bytes 2048 | tf_op jit(solution)/shard_map/psum | solution.py:183
  315.5 64.6 %all-gather.12.cloned.1.call-done = bf16[768,1536]{0,1:T(8,128)(2,1)} async-done(((bf16[768,24]{0,1:T(8,128)(2,1)}), bf16[768,1536]{0,1:T(8,128)(2,1)}) %all-gather.12.cloned.1.call-update) | async-done | bytes 2359312 | tf_op jit(solution)/shard_map/all_gather | solution.py:191
  380.1 2.5 convolution_convert_fusion
  382.6 1.2 copy.56
  383.8 23.8 %reduce-scatter.4.cloned.1.call-done = bf16[384,256]{1,0:T(8,128)(2,1)} async-done(((bf16[1536,256]{1,0:T(8,128)(2,1)}), bf16[384,256]{1,0:T(8,128)(2,1)}) %reduce-scatter.4.cloned.1.call-update) | async-done | bytes 196624
  407.5 1.7 copy.57
  (188 shorter events, 57.6 us)
Async XLA Ops:
  6.5 109.3 %copy-start.5 = (s32[64]{0:T(128)S(1)}, s32[64]{0:T(128)}, u32[]{:S(2)}) copy-start(s32[64]{0:T(128)} %param.29) | copy-start | bytes 772
  6.5 121.9 %all-gather.8.cloned.1.call-start = ((), (), s32[]{:S(2)}) async-start(), calls=%async_computation.1 | async-start | bytes 2396160 | tf_op jit(solution)/shard_map/all_gather | solution.py:121
  8.1 216.8 %all-gather.14.cloned.1.call-start = ((), (), s32[]{:S(2)}) async-start(), calls=%async_computation.4 | async-start | bytes 12779520 | tf_op jit(solution)/shard_map/all_gather | solution.py:20
  9.2 108.0 %collective-permute-start = (bf16[256,384]{0,1:T(8,128)(2,1)S(1)}, bf16[256,384]{0,1:T(8,128)(2,1)S(1)}, u32[]{:S(2)}, u32[]{:S(2)}) collective-permute-start(bf16[256,384]{0,1:T(8,128)(2,1)S(1)} %copy.43), channel_id=1, source_target_pairs={{0,1},{1,2},{2,3},{3,0},{4,5},{5,6},{6,7},{7,4},{8,9},{9,10},{10,1... | collective-permute-start | bytes 589832 | tf_op jit(solution)/shard_map/ppermute | solution.py:95
  10.8 106.8 %collective-permute-start.1 = (bf16[256,384]{0,1:T(8,128)(2,1)S(1)}, bf16[256,384]{0,1:T(8,128)(2,1)S(1)}, u32[]{:S(2)}, u32[]{:S(2)}) collective-permute-start(bf16[256,384]{0,1:T(8,128)(2,1)S(1)} %copy.43), channel_id=1, source_target_pairs={{0,3},{1,0},{2,1},{3,2},{4,7},{5,4},{6,5},{7,6},{8,11},{9,8},{10,9... | collective-permute-start | bytes 589832 | tf_op jit(solution)/shard_map/ppermute | solution.py:102
  117.2 8.4 %collective-permute-start.2 = (bf16[256,384]{0,1:T(8,128)(2,1)S(1)}, bf16[256,384]{0,1:T(8,128)(2,1)S(1)}, u32[]{:S(2)}, u32[]{:S(2)}) collective-permute-start(bf16[256,384]{0,1:T(8,128)(2,1)S(1)} %collective-permute-done), channel_id=1, source_target_pairs={{0,1},{1,2},{2,3},{3,0},{4,5},{5,6},{6,7},{7,4},{8,9},{9,10},{10,1... | collective-permute-start | bytes 589832 | tf_op jit(solution)/shard_map/ppermute | solution.py:95
  125.7 0.9 copy-start.3
  131.0 7.1 %collective-permute-start.3 = (bf16[3,1024]{1,0:T(4,128)(2,1)S(1)}, bf16[3,1024]{1,0:T(4,128)(2,1)S(1)}, u32[]{:S(2)}, u32[]{:S(2)}) collective-permute-start(bf16[3,1024]{1,0:T(4,128)(2,1)S(1)} %fusion.40), channel_id=1, source_target_pairs={{0,4},{4,8},{8,12},{12,16},{16,20},{20,24},{24,28},{28,32},{32,36}... | collective-permute-start | bytes 18440 | tf_op jit(solution)/shard_map/ppermute | solution.py:14
  138.2 2.3 copy-start
  138.2 3.1 copy-start.1
  140.5 161.9 %all-gather.10.cloned.1.call-start = ((), (), s32[]{:S(2)}) async-start(), calls=%async_computation.2 | async-start | bytes 2396160 | tf_op jit(solution)/shard_map/all_gather | solution.py:120
  141.2 238.9 %all-gather.12.cloned.1.call-start = ((), (), s32[]{:S(2)}) async-start(), calls=%async_computation.3 | async-start | bytes 2396160 | tf_op jit(solution)/shard_map/all_gather | solution.py:191
  141.9 265.6 %reduce-scatter.4.cloned.1.call-start = ((), (), s32[]{:S(2)}) async-start(), calls=%async_computation.5 | async-start | bytes 983040
  224.8 70.1 %copy-start.4 = (f32[12]{0:T(128)S(1)}, f32[12]{0:T(128)}, u32[]{:S(2)}) copy-start(f32[12]{0:T(128)} %param.25) | copy-start | bytes 148
  296.9 83.2 %copy-start.2 = (f32[768]{0:T(1024)S(1)}, f32[768]{0:T(1024)}, u32[]{:S(2)}) copy-start(f32[768]{0:T(1024)} %param.26) | copy-start | bytes 9220
Sparse Core Ops, SparseCore 0:
  10.1 79.5 all-gather.7
  140.6 84.1 all-gather.13
  227.5 74.7 all-gather.9
  304.9 75.1 all-gather.11
  383.9 23.5 reduce-scatter.3
